TPU v7x, 32 devices: a whole 2x2x4 slice. The times are simulated.
32 devices in a mesh: row: 8 (over z, x), col: 4 (over y, core).
Axes of the slice: x: 2, y: 2, z: 4, core: 2. Of those that a mesh axis runs over, the one named last changes fastest.
Arguments:
- vertex: bfloat16 [64, 4096, 4096], P(None, 'row', 'col'), may hold values from -6 to 6
- a_factor: bfloat16 [4096, 1024], P('row', 'col'), as said below
- b_factor: bfloat16 [4096, 1024], P('col', 'row'), as said below
Outputs:
- field_factor: float32 [64, 1024], P(None, 'col')
Inputs may be any that keep to these rules, and one draw needn't show every extreme that they name: `a_factor`: entries lie within -12 / sqrt(4096) and 12 / sqrt(4096). `b_factor`: entries lie within -12 / sqrt(4096) and 12 / sqrt(4096).
All inputs are finite; a program needn't handle non-finite values.
Results may differ from a plain program's by a relative error of at most 0.0003.
Values may be sent and summed in bfloat16 or wider, within the bound.
No kernel may reach another device: no remote copies, remote signals or barrier semaphores. Data moves between devices by JAX's collectives and lax.ppermute only.
A program may use at most 128 MiB of HBM per device.

v0:
```python
import jax
import jax.numpy as jnp
from jax import lax
from jax.sharding import PartitionSpec as P

ridge_term = 0.25


def on_device(vertex, a_factor, b_factor):
    fields, p_local, q_local = vertex.shape
    rank_cols = a_factor.shape[1]
    row_rank = b_factor.shape[1]
    a_rows = lax.all_gather(a_factor, "col", axis=1, tiled=True)
    total_rank = a_rows.shape[1]
    groups = fields // 4
    stacked = vertex.reshape(groups, 4 * p_local, q_local)
    column_block = lax.all_gather(b_factor, "row", axis=1, tiled=True)
    width_now = column_block.shape[1]
    a_cols = a_rows.astype(jnp.float32)

    def one_group(slab):
        product = jnp.dot(slab, column_block, preferred_element_type=jnp.float32)
        product = product.reshape(4, p_local, width_now) * a_cols[None]
        return jnp.sum(product, axis=1)

    field_part = lax.map(one_group, stacked).reshape(fields, width_now)
    gram_part = lax.dot_general(
        b_factor, column_block, (((0,), (0,)), ((), ())), preferred_element_type=jnp.float32
    )
    joined = jnp.concatenate([field_part, gram_part], axis=0)
    m_part = joined[:fields]
    gb_part = joined[fields:]
    ga_part = lax.dot_general(
        a_factor, a_rows, (((0,), (0,)), ((), ())), preferred_element_type=jnp.float32
    )
    m_total = lax.psum(m_part, ("row", "col"))
    ga_tile = lax.psum_scatter(ga_part, "row", scatter_dimension=1, tiled=True)
    gb_tile = lax.psum_scatter(gb_part, "col", scatter_dimension=1, tiled=True)
    product_tile = ga_tile * gb_tile.T
    tiles = lax.all_gather(product_tile[None], ("row", "col"), axis=0, tiled=True)
    row_count = lax.axis_size("row")
    col_count = lax.axis_size("col")
    weight = (
        tiles.reshape(row_count, col_count, rank_cols, row_rank)
        .transpose(1, 2, 0, 3)
        .reshape(total_rank, total_rank)
    )
    weight = weight + ridge_term * jnp.eye(total_rank, dtype=jnp.float32)
    factor_lower = jnp.linalg.cholesky(weight)
    solved = jax.scipy.linalg.cho_solve((factor_lower, True), m_total.T)
    col_index = lax.axis_index("col")
    return lax.dynamic_slice_in_dim(solved.T, col_index * rank_cols, rank_cols, 1)


def solution(mesh):
    return jax.shard_map(
        on_device,
        mesh=mesh,
        in_specs=(P(None, "row", "col"), P("row", "col"), P("col", "row")),
        out_specs=P(None, "col"),
        check_vma=False,
    )
```

profile of v0, /device:TPU:0, one launch (start us, length us, event | category | flops | bytes accessed | tf_op | source)
XLA Modules:
  0.0 671.2 jit_solution(9382028890872371031)
XLA Ops:
  8.1 20.4 %all-gather.5.cloned.1.call-done = bf16[512,1024]{1,0:T(8,128)(2,1)} async-done(((bf16[512,256]{1,0:T(8,128)(2,1)}), bf16[512,1024]{1,0:T(8,128)(2,1)}) %all-gather.5.cloned.1.call-update) | async-done | bytes 1048592 | tf_op jit(solution)/shard_map/all_gather | solution.py:13
  31.5 50.2 %all-gather.7.cloned.1.call-done = bf16[1024,1024]{1,0:T(8,128)(2,1)} async-done(((bf16[1024,128]{1,0:T(8,128)(2,1)}), bf16[1024,1024]{1,0:T(8,128)(2,1)}) %all-gather.7.cloned.1.call-update) | async-done | bytes 2097168 | tf_op jit(solution)/shard_map/all_gather | solution.py:17
  85.4 61.8 %reduce-scatter.3.cloned.1.call-done = f32[256,128]{1,0:T(8,128)} async-done(((f32[256,1024]{1,0:T(8,128)}), f32[256,128]{1,0:T(8,128)}) %reduce-scatter.3.cloned.1.call-update) | async-done | bytes 131088 | tf_op jit(solution)/shard_map/reduce_scatter | solution.py:37
  147.2 23.2 %reduce-scatter.5.cloned.1.call-done = f32[128,256]{0,1:T(8,128)} async-done(((f32[128,1024]{0,1:T(8,128)}), f32[128,256]{0,1:T(8,128)}) %reduce-scatter.5.cloned.1.call-update) | async-done | bytes 131088 | tf_op jit(solution)/shard_map/reduce_scatter | solution.py:38
  172.1 123.0 %while.11 = (s32[]{:T(128)}, f32[16,4,1024]{2,1,0:T(4,128)S(1)}, bf16[16,2048,1024]{2,1,0:T(8,128)(2,1)}, bf16[1024,1024]{1,0:T(8,128)(2,1)}, f32[512,1024]{1,0:T(8,128)S(1)}, /*index=5*/s32[]{:T(128)}) while((s32[]{:T(128)}, f32[16,4,1024]{2,1,0:T(4,128)S(1)}, bf16[16,2048,1024]{2,1,0:T(8,128)(2,1)}, bf16[1024,1024]{1,0:T(8,128)(2,1)}, ...), condition=%wide.region_20.21_spmd, body=%wide.region_18.20_spmd.sunk | while | flops 4299157504 | bytes 25215088 | solution.py:26
  175.0 4.8 multiply_reduce_fusion.2
  182.7 4.8 multiply_reduce_fusion.2
  190.4 4.8 multiply_reduce_fusion.2
  198.1 4.8 multiply_reduce_fusion.2
  205.8 4.8 multiply_reduce_fusion.2
  221.1 4.8 multiply_reduce_fusion.2
  236.6 4.8 multiply_reduce_fusion.2
  296.0 5.2 copy.5
  308.7 5.8 copy.6
  321.0 11.7 %cholesky.222 = f32[128,128]{1,0:T(8,128)S(1)} custom-call(f32[128,128]{1,0:T(8,128)S(1)} %cholesky.577), custom_call_target="Cholesky" | custom-call | tf_op jit(solution)/shard_map/jit(cholesky)/cholesky | solution.py:49
  332.8 9.8 %custom-call.66 = f32[1,128,128]{1,2,0:T(8,128)S(1)} custom-call(f32[1,128,128]{2,1,0:T(8,128)S(1)} %get-tuple-element.78), custom_call_target="InvertDiagBlocksLowerTriangular" | custom-call | tf_op jit(solution)/shard_map/jit(cholesky)/cholesky | solution.py:49
  346.0 11.7 %cholesky.243 = f32[128,128]{1,0:T(8,128)S(1)} custom-call(f32[128,128]{1,0:T(8,128)S(1)} %cholesky.581), custom_call_target="Cholesky" | custom-call | tf_op jit(solution)/shard_map/jit(cholesky)/cholesky | solution.py:49
  358.0 9.8 %custom-call.67 = f32[1,128,128]{1,2,0:T(8,128)S(1)} custom-call(f32[1,128,128]{2,1,0:T(8,128)S(1)} %get-tuple-element.76), custom_call_target="InvertDiagBlocksLowerTriangular" | custom-call | tf_op jit(solution)/shard_map/jit(cholesky)/cholesky | solution.py:49
  373.3 11.7 %cholesky.466 = f32[128,128]{1,0:T(8,128)S(1)} custom-call(f32[128,128]{1,0:T(8,128)S(1)} %cholesky.586), custom_call_target="Cholesky" | custom-call | tf_op jit(solution)/shard_map/jit(cholesky)/cholesky | solution.py:49
  385.8 9.8 %custom-call.68 = f32[1,128,128]{1,2,0:T(8,128)S(1)} custom-call(f32[1,128,128]{2,1,0:T(8,128)S(1)} %get-tuple-element.74), custom_call_target="InvertDiagBlocksLowerTriangular" | custom-call | tf_op jit(solution)/shard_map/jit(cholesky)/cholesky | solution.py:49
  400.2 11.7 %cholesky.485 = f32[128,128]{1,0:T(8,128)S(1)} custom-call(f32[128,128]{1,0:T(8,128)S(1)} %cholesky.591), custom_call_target="Cholesky" | custom-call | tf_op jit(solution)/shard_map/jit(cholesky)/cholesky | solution.py:49
  412.7 9.8 %custom-call.69 = f32[1,128,128]{1,2,0:T(8,128)S(1)} custom-call(f32[1,128,128]{2,1,0:T(8,128)S(1)} %get-tuple-element.72), custom_call_target="InvertDiagBlocksLowerTriangular" | custom-call | tf_op jit(solution)/shard_map/jit(cholesky)/cholesky | solution.py:49
  426.8 12.1 %cholesky.504 = f32[128,128]{1,0:T(8,128)S(1)} custom-call(f32[128,128]{1,0:T(8,128)S(1)} %cholesky.596), custom_call_target="Cholesky" | custom-call | tf_op jit(solution)/shard_map/jit(cholesky)/cholesky | solution.py:49
  439.7 9.8 %custom-call.70 = f32[1,128,128]{1,2,0:T(8,128)S(1)} custom-call(f32[1,128,128]{2,1,0:T(8,128)S(1)} %get-tuple-element.70), custom_call_target="InvertDiagBlocksLowerTriangular" | custom-call | tf_op jit(solution)/shard_map/jit(cholesky)/cholesky | solution.py:49
  453.7 11.7 %cholesky.524 = f32[128,128]{1,0:T(8,128)S(1)} custom-call(f32[128,128]{1,0:T(8,128)S(1)} %cholesky.601), custom_call_target="Cholesky" | custom-call | tf_op jit(solution)/shard_map/jit(cholesky)/cholesky | solution.py:49
  466.2 9.8 %custom-call.71 = f32[1,128,128]{1,2,0:T(8,128)S(1)} custom-call(f32[1,128,128]{2,1,0:T(8,128)S(1)} %get-tuple-element.68), custom_call_target="InvertDiagBlocksLowerTriangular" | custom-call | tf_op jit(solution)/shard_map/jit(cholesky)/cholesky | solution.py:49
  479.9 11.7 %cholesky.544 = f32[128,128]{1,0:T(8,128)S(1)} custom-call(f32[128,128]{1,0:T(8,128)S(1)} %cholesky.606), custom_call_target="Cholesky" | custom-call | tf_op jit(solution)/shard_map/jit(cholesky)/cholesky | solution.py:49
  492.4 9.8 %custom-call.72 = f32[1,128,128]{1,2,0:T(8,128)S(1)} custom-call(f32[1,128,128]{2,1,0:T(8,128)S(1)} %get-tuple-element.66), custom_call_target="InvertDiagBlocksLowerTriangular" | custom-call | tf_op jit(solution)/shard_map/jit(cholesky)/cholesky | solution.py:49
  505.2 11.7 %cholesky.562 = f32[128,128]{1,0:T(8,128)S(1)} custom-call(f32[128,128]{1,0:T(8,128)S(1)} %convolution_subtract_fusion.6), custom_call_target="Cholesky" | custom-call | tf_op jit(solution)/shard_map/jit(cholesky)/cholesky | solution.py:49
  527.3 4.8 select_select_fusion
  532.1 28.6 %while.12 = (s32[]{:T(128)}, f32[1024,1024]{0,1:T(8,128)}, s32[8,2]{0,1:T(2,128)S(1)}, f32[8,128,128]{2,1,0:T(8,128)}, s32[]{:T(128)}) while((s32[]{:T(128)}, f32[1024,1024]{0,1:T(8,128)}, s32[8,2]{0,1:T(2,128)S(1)}, f32[8,128,128]{2,1,0:T(8,128)}, s32[]{:T(128)}) %tuple.65), condition=%wide.while_cond, body=%wide.while_body.sunk | while | flops 2 | bytes 393329 | solution.py:50
  560.7 79.6 %custom-call.73 = f32[8,128,128]{1,2,0:T(8,128)S(1)} custom-call(f32[8,128,128]{2,1,0:T(8,128)} %get-tuple-element.40), custom_call_target="InvertDiagBlocksLowerTriangular" | custom-call | tf_op jit(solution)/shard_map/jit(_cho_solve)/triangular_solve | solution.py:50
  (254 shorter events, 203.9 us)
Async XLA Ops:
  6.5 22.0 %all-gather.5.cloned.1.call-start = ((), (), s32[]{:S(2)}) async-start(), calls=%async_computation.2 | async-start | bytes 1310720 | tf_op jit(solution)/shard_map/all_gather | solution.py:13
  7.3 74.4 %all-gather.7.cloned.1.call-start = ((), (), s32[]{:S(2)}) async-start(), calls=%async_computation.4 | async-start | bytes 2359296 | tf_op jit(solution)/shard_map/all_gather | solution.py:17
  8.0 139.2 %reduce-scatter.3.cloned.1.call-start = ((), (), s32[]{:S(2)}) async-start(), calls=%async_computation.3 | async-start | bytes 1179648 | tf_op jit(solution)/shard_map/reduce_scatter | solution.py:37
  28.5 56.7 %copy-start.3 = (bf16[512,1024]{1,0:T(8,128)(2,1)S(1)}, bf16[512,1024]{1,0:T(8,128)(2,1)}, u32[]{:S(2)}) copy-start(bf16[512,1024]{1,0:T(8,128)(2,1)} %all-gather.5.cloned.1.call-done) | copy-start | bytes 3145732
  31.4 139.0 %reduce-scatter.5.cloned.1.call-start = ((), (), s32[]{:S(2)}) async-start(), calls=%async_computation.5 | async-start | bytes 655360 | tf_op jit(solution)/shard_map/reduce_scatter | solution.py:38
  85.1 210.9 %all-gather.9.cloned.1.call-start = ((), (), s32[]{:S(2)}) async-start(), calls=%async_computation.7 | async-start | bytes 4325376 | tf_op jit(solution)/shard_map/all_gather | solution.py:40
  172.0 468.3 %all-reduce.3.cloned.1.call-start = ((), (), s32[]{:S(2)}) async-start(), calls=%async_computation.6 | async-start | bytes 524288 | tf_op jit(solution)/shard_map/psum | solution.py:36
  172.1 2.9 copy-start.4
  179.8 3.0 copy-start.4
  187.6 2.9 copy-start.4
  195.2 2.9 copy-start.4
  202.9 2.9 copy-start.4
  210.6 2.9 copy-start.4
  218.3 2.9 copy-start.4
  226.0 2.9 copy-start.4
  233.7 2.9 copy-start.4
  241.4 2.9 copy-start.4
  249.1 2.9 copy-start.4
  256.8 2.9 copy-start.4
  264.5 2.9 copy-start.4
  272.1 2.9 copy-start.4
  279.8 2.9 copy-start.4
  287.5 2.9 copy-start.4
  304.4 1.9 copy-start.1
  319.0 1.9 copy-start.2
  368.9 2.0 copy-start
Sparse Core Ops, SparseCore 0:
  8.9 19.5 all-gather.4
  30.5 51.0 all-gather.6
  85.0 62.1 reduce-scatter.2
  149.7 20.6 reduce-scatter.4
  173.1 62.0 all-gather.8
  296.1 125.8 all-reduce.2
where the time goes:
time: 678 us; the launch traced here: 671 us
  other arithmetic  261 us (38%)
  waiting for transfers between devices  157 us (23%)
  matrix products  131 us (19%)
  local copies, waits for them, and re-layouts  102 us (15%)
  between operations  19.4 us (3%)
    another operation x30, other arithmetic, on_device(): factor_lower = jnp.linalg.cholesky(weight)  168 us
    another operation x3, other arithmetic, on_device(): solved = jax.scipy.linalg.cho_solve((factor_lower, True), m_total.T)  84.4 us
    dot_general x16, matrix products, one_group(): product = jnp.dot(slab, column_block, preferred_element_type=jnp.float32)  76.5 us
    reduce_scatter x1, waiting for transfers between devices, on_device(): ga_tile = lax.psum_scatter(ga_part, 'row', scatter_dimension=1, tiled=True)  61.8 us
    all_gather x1, waiting for transfers between devices, on_device(): column_block = lax.all_gather(b_factor, 'row', axis=1, tiled=True)  50.2 us
    dynamic_slice x16, local copies, waits for them, and re-layouts, on_device(): field_part = lax.map(one_group, stacked).reshape(fields, width_now)  44.7 us
    another operation x40, local copies, waits for them, and re-layouts  28.5 us
    another operation x14, matrix products, on_device(): factor_lower = jnp.linalg.cholesky(weight)  25.9 us
  transfers between devices with their start and end apart: 6, of which 4 were waited for; matrix products, arithmetic and copies ran while one was open for 69% of the time, Pallas kernels for 0%

commit v1 on v0

--- a/solution.py
+++ b/solution.py
@@ -14,7 +14,16 @@
     total_rank = a_rows.shape[1]
     groups = fields // 4
     stacked = vertex.reshape(groups, 4 * p_local, q_local)
-    column_block = lax.all_gather(b_factor, "row", axis=1, tiled=True)
+    ways = lax.axis_size("row")
+    up = [(d, (d + 1) % ways) for d in range(ways)]
+    down = [(d, (d - 1) % ways) for d in range(ways)]
+    earlier, later = ([b_factor], [b_factor])
+    for _ in range(ways // 2):
+        earlier.append(lax.ppermute(earlier[-1], "row", up))
+    for _ in range((ways - 1) // 2):
+        later.append(lax.ppermute(later[-1], "row", down))
+    line = jnp.concatenate([*earlier[::-1], *later[1:]], axis=1)
+    column_block = jnp.roll(line, (lax.axis_index("row") - ways // 2) * b_factor.shape[1], axis=1)
     width_now = column_block.shape[1]
     a_cols = a_rows.astype(jnp.float32)
 

time: 678 us -> 654 us (0.965)
  waiting for transfers between devices: 157 us -> 109 us
  starting transfers between devices: 0.2 us -> 27.2 us
    all_gather x1 -> x0, waiting for transfers between devices: 50.2 us -> none  [on_device(): column_block = lax.all_gather(b_factor, 'row', axis=1, tiled=True)]
    ppermute x0 -> x7, starting transfers between devices: none -> 27.1 us  [the longest x3 19.2 us: on_device(): later.append(lax.ppermute(later[-1], 'row', down))]
    ppermute x0 -> x7, waiting for transfers between devices: none -> 22.7 us  [the longest x4 21.6 us: on_device(): earlier.append(lax.ppermute(earlier[-1], 'row', up))]
    all_gather x1, waiting for transfers between devices: 20.4 us -> 0.02 us  [on_device(): a_rows = lax.all_gather(a_factor, 'col', axis=1, tiled=True)]
  transfers between devices with their start and end apart: 6 -> 12, of which waited for: 4 -> 7; matrix products, arithmetic and copies ran while one was open for 69% -> 71% of each run, Pallas kernels for 0% -> 0%
where the time goes in v1:
time: 654 us; the launch traced here: 646 us
  other arithmetic  263 us (40%)
  matrix products  128 us (20%)
  waiting for transfers between devices  109 us (17%)
  local copies, waits for them, and re-layouts  99.4 us (15%)
  starting transfers between devices  27.2 us (4%)
  between operations  19.2 us (3%)
    another operation x30, other arithmetic, on_device(): factor_lower = jnp.linalg.cholesky(weight)  168 us
    another operation x3, other arithmetic, on_device(): solved = jax.scipy.linalg.cho_solve((factor_lower, True), m_total.T)  83.6 us
    dot_general x16, matrix products, one_group(): product = jnp.dot(slab, column_block, preferred_element_type=jnp.float32)  75.4 us
    reduce_scatter x1, waiting for transfers between devices, on_device(): ga_tile = lax.psum_scatter(ga_part, 'row', scatter_dimension=1, tiled=True)  67.7 us
    dynamic_slice x16, local copies, waits for them, and re-layouts, on_device(): field_part = lax.map(one_group, stacked).reshape(fields, width_now)  44.7 us
    another operation x14, matrix products, on_device(): factor_lower = jnp.linalg.cholesky(weight)  25.9 us
    another operation x40, local copies, waits for them, and re-layouts  23.6 us
    another operation x30, matrix products, on_device(): solved = jax.scipy.linalg.cho_solve((factor_lower, True), m_total.T)  22.6 us
  transfers between devices with their start and end apart: 12, of which 7 were waited for; matrix products, arithmetic and copies ran while one was open for 71% of the time, Pallas kernels for 0%

profile of v1, /device:TPU:0, one launch (start us, length us, event | category | flops | bytes accessed | tf_op | source)
XLA Modules:
  0.0 646.4 jit_solution(7048370617202390126)
XLA Ops:
  9.5 9.6 %collective-permute-done = bf16[1024,128]{1,0:T(8,128)(2,1)S(1)} collective-permute-done((bf16[1024,128]{1,0:T(8,128)(2,1)}, bf16[1024,128]{1,0:T(8,128)(2,1)S(1)}, u32[]{:S(2)}, u32[]{:S(2)}) %collective-permute-start) | collective-permute-done | bytes 262176 | tf_op jit(solution)/shard_map/ppermute | solution.py:22
  19.1 4.7 collective-permute-start.4
  23.8 6.2 collective-permute-done.1
  32.5 6.6 %collective-permute-start.5 = (bf16[1024,128]{1,0:T(8,128)(2,1)S(1)}, bf16[1024,128]{1,0:T(8,128)(2,1)S(1)}, u32[]{:S(2)}, u32[]{:S(2)}) collective-permute-start(bf16[1024,128]{1,0:T(8,128)(2,1)S(1)} %collective-permute-done.4), channel_id=1, source_target_pairs={{0,28},{4,0},{8,4},{12,8},{16,12},{20,16},{24,20},{28,24},{1,29},{... | collective-permute-start | bytes 786440 | tf_op jit(solution)/shard_map/ppermute | solution.py:24
  45.1 7.8 %collective-permute-start.6 = (bf16[1024,128]{1,0:T(8,128)(2,1)S(1)}, bf16[1024,128]{1,0:T(8,128)(2,1)S(1)}, u32[]{:S(2)}, u32[]{:S(2)}) collective-permute-start(bf16[1024,128]{1,0:T(8,128)(2,1)S(1)} %collective-permute-done.5), channel_id=1, source_target_pairs={{0,28},{4,0},{8,4},{12,8},{16,12},{20,16},{24,20},{28,24},{1,29},{... | collective-permute-start | bytes 786440 | tf_op jit(solution)/shard_map/ppermute | solution.py:24
  66.4 18.5 %reduce-scatter.5.cloned.1.call-done = f32[128,256]{0,1:T(8,128)} async-done(((f32[128,1024]{0,1:T(8,128)}), f32[128,256]{0,1:T(8,128)}) %reduce-scatter.5.cloned.1.call-update) | async-done | bytes 131088 | tf_op jit(solution)/shard_map/reduce_scatter | solution.py:47
  84.8 67.7 %reduce-scatter.3.cloned.1.call-done = f32[256,128]{1,0:T(8,128)} async-done(((f32[256,1024]{1,0:T(8,128)}), f32[256,128]{1,0:T(8,128)}) %reduce-scatter.3.cloned.1.call-update) | async-done | bytes 131088 | tf_op jit(solution)/shard_map/reduce_scatter | solution.py:46
  154.2 122.0 %while.11 = (s32[]{:T(128)}, f32[16,4,1024]{2,1,0:T(4,128)S(1)}, bf16[16,2048,1024]{2,1,0:T(8,128)(2,1)}, bf16[1024,1024]{1,0:T(8,128)(2,1)S(1)}, f32[512,1024]{1,0:T(8,128)}, /*index=5*/s32[]{:T(128)}) while((s32[]{:T(128)}, f32[16,4,1024]{2,1,0:T(4,128)S(1)}, bf16[16,2048,1024]{2,1,0:T(8,128)(2,1)}, bf16[1024,1024]{1,0:T(8,128)(2,1)S(1)}, ...), condition=%wide.region_20.21_spmd, body=%wide.region_18.20_spmd.sunk | while | flops 4299157504 | bytes 25215088 | solution.py:35
  157.1 4.7 multiply_reduce_fusion.2
  187.7 4.7 multiply_reduce_fusion.2
  203.0 4.7 multiply_reduce_fusion.2
  271.5 4.7 multiply_reduce_fusion.2
  277.1 5.2 copy.4
  289.8 5.8 copy.5
  302.1 11.7 %cholesky.222 = f32[128,128]{1,0:T(8,128)S(1)} custom-call(f32[128,128]{1,0:T(8,128)S(1)} %cholesky.577), custom_call_target="Cholesky" | custom-call | tf_op jit(solution)/shard_map/jit(cholesky)/cholesky | solution.py:58
  313.9 9.8 %custom-call.66 = f32[1,128,128]{1,2,0:T(8,128)S(1)} custom-call(f32[1,128,128]{2,1,0:T(8,128)S(1)} %get-tuple-element.78), custom_call_target="InvertDiagBlocksLowerTriangular" | custom-call | tf_op jit(solution)/shard_map/jit(cholesky)/cholesky | solution.py:58
  327.1 11.7 %cholesky.243 = f32[128,128]{1,0:T(8,128)S(1)} custom-call(f32[128,128]{1,0:T(8,128)S(1)} %cholesky.581), custom_call_target="Cholesky" | custom-call | tf_op jit(solution)/shard_map/jit(cholesky)/cholesky | solution.py:58
  339.1 9.8 %custom-call.67 = f32[1,128,128]{1,2,0:T(8,128)S(1)} custom-call(f32[1,128,128]{2,1,0:T(8,128)S(1)} %get-tuple-element.76), custom_call_target="InvertDiagBlocksLowerTriangular" | custom-call | tf_op jit(solution)/shard_map/jit(cholesky)/cholesky | solution.py:58
  354.4 11.7 %cholesky.466 = f32[128,128]{1,0:T(8,128)S(1)} custom-call(f32[128,128]{1,0:T(8,128)S(1)} %cholesky.586), custom_call_target="Cholesky" | custom-call | tf_op jit(solution)/shard_map/jit(cholesky)/cholesky | solution.py:58
  366.9 9.8 %custom-call.68 = f32[1,128,128]{1,2,0:T(8,128)S(1)} custom-call(f32[1,128,128]{2,1,0:T(8,128)S(1)} %get-tuple-element.74), custom_call_target="InvertDiagBlocksLowerTriangular" | custom-call | tf_op jit(solution)/shard_map/jit(cholesky)/cholesky | solution.py:58
  381.3 11.7 %cholesky.485 = f32[128,128]{1,0:T(8,128)S(1)} custom-call(f32[128,128]{1,0:T(8,128)S(1)} %cholesky.591), custom_call_target="Cholesky" | custom-call | tf_op jit(solution)/shard_map/jit(cholesky)/cholesky | solution.py:58
  393.8 9.8 %custom-call.69 = f32[1,128,128]{1,2,0:T(8,128)S(1)} custom-call(f32[1,128,128]{2,1,0:T(8,128)S(1)} %get-tuple-element.72), custom_call_target="InvertDiagBlocksLowerTriangular" | custom-call | tf_op jit(solution)/shard_map/jit(cholesky)/cholesky | solution.py:58
  407.9 12.1 %cholesky.504 = f32[128,128]{1,0:T(8,128)S(1)} custom-call(f32[128,128]{1,0:T(8,128)S(1)} %cholesky.596), custom_call_target="Cholesky" | custom-call | tf_op jit(solution)/shard_map/jit(cholesky)/cholesky | solution.py:58
  420.8 9.8 %custom-call.70 = f32[1,128,128]{1,2,0:T(8,128)S(1)} custom-call(f32[1,128,128]{2,1,0:T(8,128)S(1)} %get-tuple-element.70), custom_call_target="InvertDiagBlocksLowerTriangular" | custom-call | tf_op jit(solution)/shard_map/jit(cholesky)/cholesky | solution.py:58
  434.8 11.7 %cholesky.524 = f32[128,128]{1,0:T(8,128)S(1)} custom-call(f32[128,128]{1,0:T(8,128)S(1)} %cholesky.601), custom_call_target="Cholesky" | custom-call | tf_op jit(solution)/shard_map/jit(cholesky)/cholesky | solution.py:58
  447.3 9.8 %custom-call.71 = f32[1,128,128]{1,2,0:T(8,128)S(1)} custom-call(f32[1,128,128]{2,1,0:T(8,128)S(1)} %get-tuple-element.68), custom_call_target="InvertDiagBlocksLowerTriangular" | custom-call | tf_op jit(solution)/shard_map/jit(cholesky)/cholesky | solution.py:58
  461.0 11.7 %cholesky.544 = f32[128,128]{1,0:T(8,128)S(1)} custom-call(f32[128,128]{1,0:T(8,128)S(1)} %cholesky.606), custom_call_target="Cholesky" | custom-call | tf_op jit(solution)/shard_map/jit(cholesky)/cholesky | solution.py:58
  473.5 9.8 %custom-call.72 = f32[1,128,128]{1,2,0:T(8,128)S(1)} custom-call(f32[1,128,128]{2,1,0:T(8,128)S(1)} %get-tuple-element.66), custom_call_target="InvertDiagBlocksLowerTriangular" | custom-call | tf_op jit(solution)/shard_map/jit(cholesky)/cholesky | solution.py:58
  486.3 11.7 %cholesky.562 = f32[128,128]{1,0:T(8,128)S(1)} custom-call(f32[128,128]{1,0:T(8,128)S(1)} %convolution_subtract_fusion.6), custom_call_target="Cholesky" | custom-call | tf_op jit(solution)/shard_map/jit(cholesky)/cholesky | solution.py:58
  508.4 4.8 select_select_fusion
  513.2 23.9 %while.12 = (s32[]{:T(128)}, f32[1024,1024]{0,1:T(8,128)}, s32[8,2]{0,1:T(2,128)S(1)}, f32[8,128,128]{2,1,0:T(8,128)S(1)}, s32[]{:T(128)}) while((s32[]{:T(128)}, f32[1024,1024]{0,1:T(8,128)}, s32[8,2]{0,1:T(2,128)S(1)}, f32[8,128,128]{2,1,0:T(8,128)S(1)}, s32[]{:T(128)}) %tuple.65), condition=%wide.while_cond, body=%wide.while_body.sunk | while | flops 2 | bytes 393329 | solution.py:59
  537.1 78.8 %custom-call.73 = f32[8,128,128]{1,2,0:T(8,128)S(1)} custom-call(f32[8,128,128]{2,1,0:T(8,128)S(1)} %get-tuple-element.40), custom_call_target="InvertDiagBlocksLowerTriangular" | custom-call | tf_op jit(solution)/shard_map/jit(_cho_solve)/triangular_solve | solution.py:59
  (284 shorter events, 228.9 us)
Async XLA Ops:
  6.5 51.9 %copy-start.3 = (bf16[1024,128]{1,0:T(8,128)(2,1)S(1)}, bf16[1024,128]{1,0:T(8,128)(2,1)}, u32[]{:S(2)}) copy-start(bf16[1024,128]{1,0:T(8,128)(2,1)} %param.7) | copy-start | bytes 786436
  6.5 54.2 %all-gather.4.cloned.1.call-start = ((), (), s32[]{:S(2)}) async-start(), calls=%async_computation.2 | async-start | bytes 1310720 | tf_op jit(solution)/shard_map/all_gather | solution.py:13
  6.5 12.6 %collective-permute-start = (bf16[1024,128]{1,0:T(8,128)(2,1)}, bf16[1024,128]{1,0:T(8,128)(2,1)S(1)}, u32[]{:S(2)}, u32[]{:S(2)}) collective-permute-start(bf16[1024,128]{1,0:T(8,128)(2,1)} %param.7), channel_id=1, source_target_pairs={{0,4},{4,8},{8,12},{12,16},{16,20},{20,24},{24,28},{28,0},{1,5},{5... | collective-permute-start | bytes 786440 | tf_op jit(solution)/shard_map/ppermute | solution.py:22
  19.1 10.9 %collective-permute-start.1 = (bf16[1024,128]{1,0:T(8,128)(2,1)S(1)}, bf16[1024,128]{1,0:T(8,128)(2,1)S(1)}, u32[]{:S(2)}, u32[]{:S(2)}) collective-permute-start(bf16[1024,128]{1,0:T(8,128)(2,1)S(1)} %collective-permute-done), channel_id=1, source_target_pairs={{0,4},{4,8},{8,12},{12,16},{16,20},{20,24},{24,28},{28,0},{1,5},{5... | collective-permute-start | bytes 786440 | tf_op jit(solution)/shard_map/ppermute | solution.py:22
  19.1 13.4 %collective-permute-start.4 = (bf16[1024,128]{1,0:T(8,128)(2,1)}, bf16[1024,128]{1,0:T(8,128)(2,1)S(1)}, u32[]{:S(2)}, u32[]{:S(2)}) collective-permute-start(bf16[1024,128]{1,0:T(8,128)(2,1)} %param.7), channel_id=1, source_target_pairs={{0,28},{4,0},{8,4},{12,8},{16,12},{20,16},{24,20},{28,24},{1,29},{... | collective-permute-start | bytes 786440 | tf_op jit(solution)/shard_map/ppermute | solution.py:24
  30.0 12.5 %collective-permute-start.2 = (bf16[1024,128]{1,0:T(8,128)(2,1)S(1)}, bf16[1024,128]{1,0:T(8,128)(2,1)S(1)}, u32[]{:S(2)}, u32[]{:S(2)}) collective-permute-start(bf16[1024,128]{1,0:T(8,128)(2,1)S(1)} %collective-permute-done.1), channel_id=1, source_target_pairs={{0,4},{4,8},{8,12},{12,16},{16,20},{20,24},{24,28},{28,0},{1,5},{5... | collective-permute-start | bytes 786440 | tf_op jit(solution)/shard_map/ppermute | solution.py:22
  32.5 12.6 %collective-permute-start.5 = (bf16[1024,128]{1,0:T(8,128)(2,1)S(1)}, bf16[1024,128]{1,0:T(8,128)(2,1)S(1)}, u32[]{:S(2)}, u32[]{:S(2)}) collective-permute-start(bf16[1024,128]{1,0:T(8,128)(2,1)S(1)} %collective-permute-done.4), channel_id=1, source_target_pairs={{0,28},{4,0},{8,4},{12,8},{16,12},{20,16},{24,20},{28,24},{1,29},{... | collective-permute-start | bytes 786440 | tf_op jit(solution)/shard_map/ppermute | solution.py:24
  42.5 12.8 %collective-permute-start.3 = (bf16[1024,128]{1,0:T(8,128)(2,1)S(1)}, bf16[1024,128]{1,0:T(8,128)(2,1)S(1)}, u32[]{:S(2)}, u32[]{:S(2)}) collective-permute-start(bf16[1024,128]{1,0:T(8,128)(2,1)S(1)} %collective-permute-done.2), channel_id=1, source_target_pairs={{0,4},{4,8},{8,12},{12,16},{16,20},{20,24},{24,28},{28,0},{1,5},{5... | collective-permute-start | bytes 786440 | tf_op jit(solution)/shard_map/ppermute | solution.py:22
  45.0 39.8 %reduce-scatter.5.cloned.1.call-start = ((), (), s32[]{:S(2)}) async-start(), calls=%async_computation.4 | async-start | bytes 655360 | tf_op jit(solution)/shard_map/reduce_scatter | solution.py:47
  45.1 12.9 %collective-permute-start.6 = (bf16[1024,128]{1,0:T(8,128)(2,1)S(1)}, bf16[1024,128]{1,0:T(8,128)(2,1)S(1)}, u32[]{:S(2)}, u32[]{:S(2)}) collective-permute-start(bf16[1024,128]{1,0:T(8,128)(2,1)S(1)} %collective-permute-done.5), channel_id=1, source_target_pairs={{0,28},{4,0},{8,4},{12,8},{16,12},{20,16},{24,20},{28,24},{1,29},{... | collective-permute-start | bytes 786440 | tf_op jit(solution)/shard_map/ppermute | solution.py:24
  60.7 91.9 %reduce-scatter.3.cloned.1.call-start = ((), (), s32[]{:S(2)}) async-start(), calls=%async_computation.3 | async-start | bytes 1179648 | tf_op jit(solution)/shard_map/reduce_scatter | solution.py:46
  63.5 213.6 %all-gather.6.cloned.1.call-start = ((), (), s32[]{:S(2)}) async-start(), calls=%async_computation.6 | async-start | bytes 4325376 | tf_op jit(solution)/shard_map/all_gather | solution.py:49
  154.2 461.8 %all-reduce.3.cloned.1.call-start = ((), (), s32[]{:S(2)}) async-start(), calls=%async_computation.5 | async-start | bytes 524288 | tf_op jit(solution)/shard_map/psum | solution.py:45
  154.2 2.9 copy-start.4
  161.9 2.9 copy-start.4
  169.5 2.9 copy-start.4
  177.2 3.0 copy-start.4
  184.9 2.9 copy-start.4
  192.5 2.9 copy-start.4
  200.1 2.9 copy-start.4
  207.7 2.9 copy-start.4
  215.4 2.9 copy-start.4
  223.0 2.9 copy-start.4
  230.6 2.9 copy-start.4
  238.2 2.9 copy-start.4
  245.8 2.9 copy-start.4
  253.5 2.9 copy-start.4
  261.1 2.9 copy-start.4
  268.7 2.9 copy-start.4
  285.5 1.9 copy-start.1
  300.2 1.9 copy-start.2
  350.0 2.0 copy-start
  (1 other events, 1.9 us)
Sparse Core Ops, SparseCore 0:
  45.1 15.5 all-gather.3
  63.2 21.6 reduce-scatter.4
  88.6 63.8 reduce-scatter.2
  155.3 61.0 all-gather.5
  277.2 124.6 all-reduce.2
